TPU v7x, 256 devices: a whole 4x4x8 slice. The times are simulated.
256 devices in a mesh: grp: 8 (over x, core), row: 32 (over y, z).
Axes of the slice: x: 4, y: 4, z: 8, core: 2. Of those that a mesh axis runs over, the one named last changes fastest.
Arguments:
- matrix: float32 [524288, 512], P(('grp', 'row')), may hold values from -1 to 1
- targets: float32 [524288, 128], P(('grp', 'row')), may hold values from -8 to 8
- sign_bits: int32 [524288], P(('grp', 'row')), may hold values from 0 to 1
- picked_rows: int32 [256, 1024], P(('grp', 'row')), may hold values from 0 to 2047, as said below
Outputs:
- factor: float32 [512, 512], replicated
- solution: float32 [512, 128], replicated
- residual: float32 [524288, 128], P(('grp', 'row'))
Inputs may be any that keep to these rules, and one draw needn't show every extreme that they name: Each row of picked_rows holds 1024 different numbers.
All inputs are finite; a program needn't handle non-finite values.
Results may differ from a plain program's by a relative error of at most 0.0003.
Values sent between devices are 32-bit elements; how exact they have to be, the bound alone decides.
No kernel may reach another device: no remote copies, remote signals or barrier semaphores. Data moves between devices by JAX's collectives and lax.ppermute only.
A program may use at most 64 MiB of HBM per device.

v0:
```python
import jax
import jax.numpy as jnp
from jax import lax
from jax.experimental import pallas as pl
from jax.experimental.pallas import tpu as pltpu
from jax.sharding import PartitionSpec as P

N = 512
NRHS = 128
SK = 1024
ROWS_DEV = 2048
ITERS = 2
NB = 128
UNITS = 128
TALL = 24
HI = lax.Precision.HIGHEST
F32 = jnp.float32
BF16 = jnp.bfloat16
V = pltpu.VMEM
NN = (((1,), (0,)), ((), ()))
TN = (((0,), (0,)), ((), ()))
MIB = 1 << 20
LOWER = [(i, j) for i in range(4) for j in range(i + 1)]


def core():
    return lax.rem(lax.axis_index("grp"), 2)


def shape(*dims):
    return jax.ShapeDtypeStruct(dims, F32)


def split(v):
    hi = v.astype(BF16)
    return hi, (v - hi.astype(F32)).astype(BF16)


def dot(a, b, dims=NN):
    return lax.dot_general(a, b, dims, preferred_element_type=F32)


def dot_hi(a, b, dims=NN):
    return lax.dot_general(a, b, dims, precision=HI, preferred_element_type=F32)


def parity(v, bits):
    shift = 8
    while shift:
        if shift < bits:
            v = v ^ (v >> shift)
        shift //= 2
    return v & 1


def terms_body(a_ref, t_ref, sign_ref, pick_ref, keep_ref, send_ref, base_ref, high_ref, acc_ref, nacc_ref, p_ref):
    k = pl.program_id(0)
    depth = a_ref.shape[0]

    @pl.when(k == 0)
    def _():
        lane = lax.broadcasted_iota(jnp.int32, (NB, depth), 1)
        for b in range(SK // NB):
            row = pick_ref[0:1, b * NB : (b + 1) * NB]
            col = jnp.broadcast_to(row, (NB, NB)).T
            both = jnp.concatenate([col] * (depth // NB), axis=1)
            base_ref[b * NB : (b + 1) * NB, :] = (1 - 2 * parity(both & (depth - 1) & lane, 8)).astype(F32).astype(BF16)
            high_ref[b * NB : (b + 1) * NB, :] = col >> 8
        acc_ref[...] = jnp.zeros_like(acc_ref)
        nacc_ref[...] = jnp.zeros_like(nacc_ref)

    flips = jnp.concatenate([sign_ref[pl.ds(2 * k, 1), :], sign_ref[pl.ds(2 * k + 1, 1), :]], axis=1)
    flips = (1 - 2 * flips).astype(F32)
    hi, lo = split(a_ref[...])
    for b in range(SK // NB):
        rows = slice(b * NB, (b + 1) * NB)
        turn = (1 - 2 * parity(high_ref[rows, :] & k, 4)).astype(F32)
        turn = jnp.concatenate([turn] * (depth // NB), axis=1) * flips
        h = base_ref[rows, :] * turn.astype(BF16)
        acc_ref[rows, :] += dot(h, hi) + dot(h, lo)

    thi, tlo = split(t_ref[...])
    his, los = jnp.concatenate([thi, hi], axis=1), jnp.concatenate([tlo, lo], axis=1)
    hit, lot = hi.T, lo.T
    for i in range(4):
        rows, wide = slice(i * NB, (i + 1) * NB), (i + 2) * NB
        nacc_ref[rows, :wide] += dot(hit[rows], his[:, :wide]) + (dot(hit[rows], los[:, :wide]) + dot(lot[rows], his[:, :wide]))

    @pl.when(k == pl.num_programs(0) - 1)
    def _():
        for i in range(4):
            p_ref[0, i] = nacc_ref[i * NB : (i + 1) * NB, :NB]
        for b, (i, j) in enumerate(LOWER):
            p_ref[(b + 4) // 8, (b + 4) % 8] = nacc_ref[i * NB : (i + 1) * NB, (j + 1) * NB : (j + 2) * NB]
        p_ref[1, 6:] = jnp.zeros_like(p_ref[1, 6:])
        for out, half in ((keep_ref, core()), (send_ref, 1 - core())):

            def put(r, _, out=out, half=half):
                rows = acc_ref[pl.ds(pl.multiple_of(half * (SK // 2) + r * 16, 16), 16), :]
                for c in range(4):
                    out[pl.ds(r * 4 + c, 1), :16, :] = rows[:, c * NB : (c + 1) * NB][None]
                block = p_ref[pl.ds(half, 1), pl.ds(r // 4, 1), pl.ds(pl.multiple_of(lax.rem(r, 4) * 32, 32), 32), :]
                out[pl.ds(r * 4, 4), 16:, :] = block.reshape(4, 8, NB)
                return 0

            lax.fori_loop(0, 32, put, 0)


def terms(matrix, targets, sign_bits, picked_rows):
    depth = 256
    whole = lambda k: (0, 0)
    return pl.pallas_call(
        terms_body,
        out_shape=[shape(UNITS, TALL, NB)] * 2,
        grid=(ROWS_DEV // depth,),
        in_specs=[
            pl.BlockSpec((depth, N), lambda k: (k, 0)),
            pl.BlockSpec((depth, NRHS), lambda k: (k, 0)),
            pl.BlockSpec((ROWS_DEV // NB, NB), whole),
            pl.BlockSpec((1, SK), whole),
        ],
        out_specs=[pl.BlockSpec((UNITS, TALL, NB), lambda k: (0, 0, 0))] * 2,
        scratch_shapes=[
            V((SK, depth), BF16),
            V((SK, NB), jnp.int32),
            V((SK, N), F32),
            V((N, N + NRHS), F32),
            V((2, 8, NB, NB), F32),
        ],
        compiler_params=pltpu.CompilerParams(vmem_limit_bytes=32 * MIB),
        name="terms",
    )(matrix, targets, sign_bits.reshape(ROWS_DEV // NB, NB), picked_rows)


def other_core(v):
    return lax.ppermute(v, "grp", [(i, i ^ 1) for i in range(8)])


def over_x(v):
    groups = [[0, 2, 4, 6], [1, 3, 5, 7]]
    return lax.all_to_all(v, "grp", 0, 0, axis_index_groups=groups, tiled=True)


def over_row(v):
    return lax.all_to_all(v, "row", 0, 0, tiled=True)


def summed(keep, send):
    v = (keep + other_core(send)).reshape(4, 32, TALL, NB)
    v = jnp.sum(over_x(v), axis=0)
    v = jnp.sum(over_row(v), axis=0)
    v = over_row(jnp.broadcast_to(v, (32, TALL, NB)))
    v = over_x(jnp.broadcast_to(v, (4, 32, TALL, NB)))
    return v.reshape(UNITS, TALL, NB)


def gram_body(in_ref, out_ref, s_ref):
    def take(r, _):
        for c in range(4):
            s_ref[pl.ds(pl.multiple_of(r * 16, 16), 16), c * NB : (c + 1) * NB] = in_ref[pl.ds(r * 4 + c, 1), :16, :][0]
        out_ref[pl.ds(pl.multiple_of(len(LOWER) * NB + r * 32, 32), 32), :] = in_ref[pl.ds(r * 4, 4), 16:, :].reshape(32, NB)
        return 0

    lax.fori_loop(0, 32, take, 0)
    hi, lo = split(s_ref[...])
    hit, lot = hi.T, lo.T
    for i in range(4):
        rows, wide = slice(i * NB, (i + 1) * NB), (i + 1) * NB
        g = dot(hit[rows], hi[:, :wide]) + (dot(hit[rows], lo[:, :wide]) + dot(lot[rows], hi[:, :wide]))
        for j in range(i + 1):
            b = LOWER.index((i, j))
            out_ref[b * NB : (b + 1) * NB, :] = g[:, j * NB : (j + 1) * NB]


def gram(v):
    return pl.pallas_call(
        gram_body,
        out_shape=shape((len(LOWER) + 8) * NB, NB),
        in_specs=[pl.BlockSpec(memory_space=V)],
        out_specs=pl.BlockSpec(memory_space=V),
        scratch_shapes=[V((SK // 2, N), F32)],
        compiler_params=pltpu.CompilerParams(vmem_limit_bytes=16 * MIB),
        name="gram",
    )(v)


def rows_of(v, k):
    return jnp.broadcast_to(v[k : k + 1, :], (8, v.shape[1]))


def lanes_of(v, j):
    return jnp.broadcast_to(v[:, j : j + 1], (8, NB))


def factor_block(d_ref, b_ref, u_ref, w_ref):
    lane = lax.broadcasted_iota(jnp.int32, (8, NB), 1)
    sub = lax.broadcasted_iota(jnp.int32, (8, NB), 0)

    def packed(vs):
        v = vs[0]
        for m in range(1, 8):
            v = jnp.where(sub == m, vs[m], v)
        return v

    for p in range(NB // 8):
        q = 8 * p
        cols = [lanes_of(d_ref[q : q + 8, :], q + m) for m in range(8)]
        s = {(k, m): rows_of(cols[m], k) for m in range(8) for k in range(m, 8)}
        l, r = {}, {}
        for m in range(8):
            r[m] = lax.rsqrt(s[m, m])
            for k in range(m + 1, 8):
                l[k, m] = s[k, m] * r[m]
            for k in range(m + 1, 8):
                for j in range(m + 1, k + 1):
                    s[k, j] = s[k, j] - l[k, m] * l[j, m]

        def forward(vs):
            out = []
            for m in range(8):
                v = vs[m]
                for k in range(m):
                    v = v - l[m, k] * out[k]
                out.append(v * r[m])
            return out

        t, tb = d_ref[q : q + 8, :], b_ref[q : q + 8, :]
        u = forward([rows_of(t, m) for m in range(8)])
        w = forward([rows_of(tb, m) for m in range(8)])
        u_ref[q : q + 8, :] = jnp.where(lane >= q + sub, packed(u), 0.0)
        w_ref[q : q + 8, :] = packed(w)
        for i in range(p + 1, NB // 8):
            o = 8 * i
            v, y = d_ref[o : o + 8, :], b_ref[o : o + 8, :]
            c = forward([lanes_of(v, q + m) for m in range(8)])
            for m in range(8):
                v = v - c[m] * u[m]
                y = y - c[m] * w[m]
            d_ref[o : o + 8, :] = v
            b_ref[o : o + 8, :] = y


def finish_body(
    gram_scale, grad_scale, own_ref, got_ref, a_hbm, t_hbm, l_ref, x_ref, r_hbm,
    a_ref, b_ref, d_ref, db_ref, w_ref, u_ref, lt_ref, li_ref, m_ref, mat_ref, t_ref, r_ref, sems,
):
    fetch = [pltpu.make_async_copy(a_hbm, mat_ref, sems.at[0]), pltpu.make_async_copy(t_hbm, t_ref, sems.at[1])]
    for copy in fetch:
        copy.start()
    zeros = jnp.zeros((NB, NB), F32)
    for b, (i, j) in enumerate(LOWER):
        rows = slice(b * NB, (b + 1) * NB)
        g = (own_ref[rows, :] + got_ref[rows, :]) * gram_scale
        a_ref[i * NB : (i + 1) * NB, j * NB : (j + 1) * NB] = g
        if i != j:
            a_ref[j * NB : (j + 1) * NB, i * NB : (i + 1) * NB] = g.T
    lt_ref[...] = jnp.zeros_like(lt_ref)
    li_ref[...] = jnp.zeros_like(li_ref)
    b_ref[...] = jnp.zeros_like(b_ref)
    row = lax.broadcasted_iota(jnp.int32, (NB, NB), 0)
    eye = (row == lax.broadcasted_iota(jnp.int32, (NB, NB), 1)).astype(F32)

    def block(step, _):
        here = pl.ds(pl.multiple_of(step * NB, NB), NB)
        d_ref[...] = a_ref[here, here]
        db_ref[...] = eye
        factor_block(d_ref, db_ref, u_ref, w_ref)
        lt_ref[here, here] = u_ref[...]
        li_ref[here, here] = w_ref[...]
        for j in range(N // NB):

            @pl.when(step == j)
            def _(j=j):
                o, e = j * NB, (j + 1) * NB
                w = w_ref[...]
                if j:
                    li_ref[o:e, 0:o] = dot_hi(w, b_ref[o:e, 0:o])
                if e < N:
                    u = dot_hi(w, a_ref[o:e, e:])
                    lt_ref[o:e, e:] = u
                    ut = u.T
                    a_ref[e:, e:] = a_ref[e:, e:] - dot_hi(ut, u)
                    b_ref[e:, 0:e] = b_ref[e:, 0:e] - dot_hi(ut, li_ref[o:e, 0:e])

        return 0

    lax.fori_loop(0, N // NB, block, 0)
    l_ref[...] = lt_ref[...].T

    base = len(LOWER) * NB

    def moment(b):
        at = pl.ds(base + (b % 8) * NB, NB)
        mine = own_ref[at, :]
        other = got_ref[at, :]
        return jnp.where(core() == b // 8, mine, other) * grad_scale

    first = jnp.concatenate([moment(i) for i in range(4)], axis=0)
    for b, (i, j) in enumerate(LOWER):
        g = moment(b + 4)
        m_ref[i * NB : (i + 1) * NB, j * NB : (j + 1) * NB] = g
        if i != j:
            m_ref[j * NB : (j + 1) * NB, i * NB : (i + 1) * NB] = g.T

    def times(parts, v):
        hi, lo = split(v)
        both = jnp.concatenate([hi, lo], axis=1)
        ahead, behind = dot(parts[0], both), dot(parts[1], both)
        return ahead[:, :NRHS] + ((ahead[:, NRHS:] + behind[:, :NRHS]) + behind[:, NRHS:])

    inverse, turned, moments = split(li_ref[...]), split(li_ref[...].T), split(m_ref[...])
    x = times(turned, times(inverse, first))
    for _ in range(ITERS - 1):
        x = x + times(turned, times(inverse, first - times(moments, x)))
    x_ref[...] = x
    for copy in fetch:
        copy.wait()
    xs = jnp.concatenate(split(x), axis=1)
    puts = []
    deep = ROWS_DEV // 4
    for c in range(4):
        rows = slice(c * deep, (c + 1) * deep)
        hi, lo = split(mat_ref[rows, :])
        ahead, behind = dot(hi, xs), dot(lo, xs)
        r_ref[rows, :] = t_ref[rows, :] - (ahead[:, :NRHS] + ((ahead[:, NRHS:] + behind[:, :NRHS]) + behind[:, NRHS:]))
        puts.append(pltpu.make_async_copy(r_ref.at[rows, :], r_hbm.at[rows, :], sems.at[2 + c]))
        puts[-1].start()
    for copy in puts:
        copy.wait()


def finished(own, got, matrix, targets, gram_scale, grad_scale):
    def body(*refs):
        finish_body(gram_scale, grad_scale, *refs)

    vmem, hbm = pl.BlockSpec(memory_space=V), pl.BlockSpec(memory_space=pl.ANY)
    return pl.pallas_call(
        body,
        out_shape=[shape(N, N), shape(N, NRHS), shape(ROWS_DEV, NRHS)],
        in_specs=[vmem, vmem, hbm, hbm],
        out_specs=[vmem, vmem, hbm],
        scratch_shapes=[V((N, N), F32)] * 2
        + [V((NB, NB), F32)] * 4
        + [V((N, N), F32)] * 3
        + [V((ROWS_DEV, N), F32)]
        + [V((ROWS_DEV, NRHS), F32)] * 2
        + [pltpu.SemaphoreType.DMA((6,))],
        compiler_params=pltpu.CompilerParams(vmem_limit_bytes=40 * MIB),
        name="finish",
    )(own, got, matrix, targets)


def on_device(matrix, targets, sign_bits, picked_rows):
    total_rows = matrix.shape[0] * lax.axis_size("grp") * lax.axis_size("row")
    keep, send = terms(matrix, targets, sign_bits, picked_rows)
    own = gram(summed(keep, send))
    return tuple(finished(own, other_core(own), matrix, targets, N / (SK * total_rows), N / total_rows))


def solution(mesh):
    rows = P(("grp", "row"), None)
    return jax.shard_map(
        on_device,
        mesh=mesh,
        in_specs=(rows, rows, P(("grp", "row")), rows),
        out_specs=(P(), P(), rows),
        check_vma=False,
    )
```

profile of v0, /device:TPU:1, one launch (start us, length us, event | category | flops | bytes accessed | tf_op | source)
XLA Modules:
  0.0 137.4 jit_solution(9578817628220046773)
XLA Ops:
  0.6 0.0 copy-start
  0.6 2.2 %copy-done = f32[2048,512]{1,0:T(8,128)S(1)} copy-done((f32[2048,512]{1,0:T(8,128)S(1)}, f32[2048,512]{1,0:T(8,128)}, u32[]{:S(2)}) %copy-start) | copy-done | bytes 4194328
  2.8 0.0 copy-start.2
  2.8 1.2 copy-done.2
  4.0 0.0 copy-start.4
  4.0 0.7 copy-done.4
  4.7 0.0 copy-start.5
  4.7 0.7 copy-done.5
  5.4 11.0 %terms.1 = (f32[128,24,128]{2,1,0:T(8,128)S(1)}, f32[128,24,128]{2,1,0:T(8,128)S(1)}) custom-call(f32[2048,512]{1,0:T(8,128)S(1)} %copy-done, f32[2048,128]{1,0:T(8,128)S(1)} %copy-done.2, s32[16,128]{1,0:T(8,128)S(1)} %bitcast.4, s32[1,1024]{1,0:T(1,128)S(1)} %copy-done.5), custom_call_target="tpu_custom_call" | custom-call | tf_op jit(solution)/shard_map/terms/pallas_call | solution.py:112
  16.4 3.3 %collective-permute-start = (f32[128,24,128]{2,1,0:T(8,128)S(1)}, f32[128,24,128]{2,1,0:T(8,128)S(1)}, u32[]{:S(2)}, u32[]{:S(2)}) collective-permute-start(f32[128,24,128]{2,1,0:T(8,128)S(1)} %get-tuple-element.6), channel_id=1, source_target_pairs={{0,32},{32,0},{64,96},{96,64},{128,160},{160,128},{192,224},{224,1... | collective-permute-start | bytes 4718600 | tf_op jit(solution)/shard_map/ppermute | solution.py:136
  19.7 3.0 %collective-permute-done = f32[128,24,128]{2,1,0:T(8,128)S(1)} collective-permute-done((f32[128,24,128]{2,1,0:T(8,128)S(1)}, f32[128,24,128]{2,1,0:T(8,128)S(1)}, u32[]{:S(2)}, u32[]{:S(2)}) %collective-permute-start) | collective-permute-done | bytes 1572896 | tf_op jit(solution)/shard_map/ppermute | solution.py:136
  22.7 0.2 add.3
  22.9 22.9 %all_to_all.20 = f32[4,32,24,128]{3,2,1,0:T(8,128)S(1)} all-to-all(f32[4,32,24,128]{3,2,1,0:T(8,128)S(1)} %bitcast.5), channel_id=1, replica_groups={{0,64,128,192},{32,96,160,224},{1,65,129,193},{33,97,161,225},{2,66,130..., dimensions={0} | all-to-all | bytes 3145728 | tf_op jit(solution)/shard_map/all_to_all | solution.py:141
  45.8 0.1 reduce_sum.18
  45.9 20.6 %all_to_all.21 = f32[32,24,128]{2,1,0:T(8,128)S(1)} all-to-all(f32[32,24,128]{2,1,0:T(8,128)S(1)} %reduce_sum.18), channel_id=1, replica_groups=mesh['grp'=8,'row'=32] {'row'}, dimensions={0} | all-to-all | bytes 786432 | tf_op jit(solution)/shard_map/all_to_all | solution.py:145
  66.6 17.4 %all_to_all.22 = f32[32,24,128]{2,1,0:T(8,128)S(1)} all-to-all(f32[32,24,128]{2,1,0:T(8,128)S(1)} %broadcast_in_dim.6), channel_id=1, replica_groups=mesh['grp'=8,'row'=32] {'row'}, dimensions={0} | all-to-all | bytes 786432 | tf_op jit(solution)/shard_map/all_to_all | solution.py:145
  84.0 0.1 broadcast_in_dim.7
  84.1 0.0 copy-start.1
  84.1 18.3 %all_to_all.23 = f32[4,32,24,128]{3,2,1,0:T(8,128)S(1)} all-to-all(f32[4,32,24,128]{3,2,1,0:T(8,128)S(1)} %broadcast_in_dim.7), channel_id=1, replica_groups={{0,64,128,192},{32,96,160,224},{1,65,129,193},{33,97,161,225},{2,66,130..., dimensions={0} | all-to-all | bytes 3145728 | tf_op jit(solution)/shard_map/all_to_all | solution.py:141
  102.4 0.0 copy-start.3
  102.4 1.0 gram.1.refs_0_
  103.5 6.4 %collective-permute-start.1 = (f32[2304,128]{1,0:T(8,128)S(1)}, f32[2304,128]{1,0:T(8,128)S(1)}, u32[]{:S(2)}, u32[]{:S(2)}) collective-permute-start(f32[2304,128]{1,0:T(8,128)S(1)} %gram.1.refs_0_), channel_id=1, source_target_pairs={{0,32},{32,0},{64,96},{96,64},{128,160},{160,128},{192,224},{224,1... | collective-permute-start | bytes 3538952 | tf_op jit(solution)/shard_map/ppermute | solution.py:136
  109.8 2.5 %collective-permute-done.1.refs_1_ = f32[2304,128]{1,0:T(8,128)S(1)} collective-permute-done((f32[2304,128]{1,0:T(8,128)S(1)}, f32[2304,128]{1,0:T(8,128)S(1)}, u32[]{:S(2)}, u32[]{:S(2)}) %collective-permute-start.1) | collective-permute-done | bytes 1179680 | tf_op jit(solution)/shard_map/ppermute | solution.py:136
  112.3 0.0 copy-done.1
  112.3 0.0 copy-done.3
  112.3 24.9 %finish.1 = (f32[512,512]{1,0:T(8,128)}, f32[512,128]{1,0:T(8,128)}, f32[2048,128]{1,0:T(8,128)}) custom-call(f32[2304,128]{1,0:T(8,128)S(1)} %gram.1.refs_0_, f32[2304,128]{1,0:T(8,128)S(1)} %collective-permute-done.1.refs_1_, f32[2048,512]{1,0:T(8,128)S(1)} %copy-done.1, f32[2048,128]{1,0:T(8,128)S(1)} %copy-done.3), custom_call_target="tpu_custom_call" | custom-call | tf_op jit(solution)/shard_map/finish/pallas_call | solution.py:337
  (2 shorter events, 0.1 us)
Async XLA Ops:
  0.6 2.2 %copy-start = (f32[2048,512]{1,0:T(8,128)S(1)}, f32[2048,512]{1,0:T(8,128)}, u32[]{:S(2)}) copy-start(f32[2048,512]{1,0:T(8,128)} %refs_2_.1) | copy-start | bytes 12582916
  2.8 1.2 copy-start.2
  4.0 0.7 copy-start.4
  4.7 0.7 copy-start.5
  16.4 6.3 %collective-permute-start = (f32[128,24,128]{2,1,0:T(8,128)S(1)}, f32[128,24,128]{2,1,0:T(8,128)S(1)}, u32[]{:S(2)}, u32[]{:S(2)}) collective-permute-start(f32[128,24,128]{2,1,0:T(8,128)S(1)} %get-tuple-element.6), channel_id=1, source_target_pairs={{0,32},{32,0},{64,96},{96,64},{128,160},{160,128},{192,224},{224,1... | collective-permute-start | bytes 4718600 | tf_op jit(solution)/shard_map/ppermute | solution.py:136
  84.1 28.2 %copy-start.1 = (f32[2048,512]{1,0:T(8,128)S(1)}, f32[2048,512]{1,0:T(8,128)}, u32[]{:S(2)}) copy-start(f32[2048,512]{1,0:T(8,128)} %refs_2_.1) | copy-start | bytes 12582916
  102.4 9.9 %copy-start.3 = (f32[2048,128]{1,0:T(8,128)S(1)}, f32[2048,128]{1,0:T(8,128)}, u32[]{:S(2)}) copy-start(f32[2048,128]{1,0:T(8,128)} %refs_3_.1) | copy-start | bytes 3145732
  103.5 8.9 %collective-permute-start.1 = (f32[2304,128]{1,0:T(8,128)S(1)}, f32[2304,128]{1,0:T(8,128)S(1)}, u32[]{:S(2)}, u32[]{:S(2)}) collective-permute-start(f32[2304,128]{1,0:T(8,128)S(1)} %gram.1.refs_0_), channel_id=1, source_target_pairs={{0,32},{32,0},{64,96},{96,64},{128,160},{160,128},{192,224},{224,1... | collective-permute-start | bytes 3538952 | tf_op jit(solution)/shard_map/ppermute | solution.py:136
where the time goes:
time: 139 us; the launch traced here: 137 us
  blocking collectives  79.2 us (57%)
  Pallas kernels  36.9 us (27%)
  starting transfers between devices  9.67 us (7%)
  waiting for transfers between devices  5.51 us (4%)
  local copies, waits for them, and re-layouts  4.93 us (4%)
    all_to_all x2, blocking collectives, over_x(): return lax.all_to_all(v, 'grp', 0, 0, axis_index_groups=groups, tiled=True)  41.1 us
    all_to_all x2, blocking collectives, over_row(): return lax.all_to_all(v, 'row', 0, 0, tiled=True)  38.1 us
    pallas_call x1, Pallas kernels, finished(): pl.pallas_call(body, out_shape=[shape(N, N), shape(N, NRHS), shape(ROWS_D...  24.9 us
    pallas_call x1, Pallas kernels, terms(): pl.pallas_call(terms_body, out_shape=[shape(UNITS, TALL, NB)] * 2, grid=(...  11 us
    ppermute x2, starting transfers between devices, other_core(): return lax.ppermute(v, 'grp', [(i, i ^ 1) for i in range(8)])  9.67 us
    ppermute x2, waiting for transfers between devices, other_core(): return lax.ppermute(v, 'grp', [(i, i ^ 1) for i in range(8)])  5.51 us
    unnamed x12, local copies, waits for them, and re-layouts  4.8 us
  transfers between devices with their start and end apart: 2, of which 2 were waited for; matrix products, arithmetic and copies ran while one was open for 0% of the time, Pallas kernels for 0%

commit v1 on v0

--- a/solution.py
+++ b/solution.py
@@ -104,6 +104,10 @@
                 return 0
 
             lax.fori_loop(0, 32, put, 0)
+
+
+def in_hbm(v):
+    return pltpu.with_memory_space_constraint(v, pltpu.HBM)
 
 
 def terms(matrix, targets, sign_bits, picked_rows):
@@ -129,28 +133,36 @@
         ],
         compiler_params=pltpu.CompilerParams(vmem_limit_bytes=32 * MIB),
         name="terms",
-    )(matrix, targets, sign_bits.reshape(ROWS_DEV // NB, NB), picked_rows)
+    )(*map(in_hbm, (matrix, targets, sign_bits.reshape(ROWS_DEV // NB, NB), picked_rows)))
 
 
 def other_core(v):
     return lax.ppermute(v, "grp", [(i, i ^ 1) for i in range(8)])
 
 
-def over_x(v):
-    groups = [[0, 2, 4, 6], [1, 3, 5, 7]]
-    return lax.all_to_all(v, "grp", 0, 0, axis_index_groups=groups, tiled=True)
-
-
-def over_row(v):
-    return lax.all_to_all(v, "row", 0, 0, tiled=True)
+def device(g, y, z):
+    return g * 32 + y * 8 + z
+
+
+def over_near(v):
+    groups = [
+        [device(2 * x + c, y, 2 * far + near) for x in range(4) for y in range(4) for near in range(2)]
+        for c in range(2)
+        for far in range(4)
+    ]
+    return lax.all_to_all(v, ("grp", "row"), 0, 0, axis_index_groups=groups, tiled=True)
+
+
+def over_far(v):
+    groups = [[8 * y + 2 * far + near for far in range(4)] for y in range(4) for near in range(2)]
+    return lax.all_to_all(v, "row", 0, 0, axis_index_groups=groups, tiled=True)
 
 
 def summed(keep, send):
-    v = (keep + other_core(send)).reshape(4, 32, TALL, NB)
-    v = jnp.sum(over_x(v), axis=0)
-    v = jnp.sum(over_row(v), axis=0)
-    v = over_row(jnp.broadcast_to(v, (32, TALL, NB)))
-    v = over_x(jnp.broadcast_to(v, (4, 32, TALL, NB)))
+    v = (keep + other_core(send)).reshape(32, 4, TALL, NB)
+    v = jnp.sum(over_near(v), axis=0)
+    v = jnp.sum(over_far(jnp.broadcast_to(v, (4, 4, TALL, NB))), axis=0)
+    v = over_near(jnp.broadcast_to(v, (32, 4, TALL, NB)))
     return v.reshape(UNITS, TALL, NB)
 
 

time: 139 us -> 121 us (0.87)
  blocking collectives: 79.2 us -> 68.1 us
  local copies, waits for them, and re-layouts: 4.93 us -> 0.2 us
  starting transfers between devices: 9.67 us -> 7.53 us
    all_to_all x4 -> x3, blocking collectives: 79.2 us -> 68.1 us  [the longest x2 53.3 us: over_near(): lax.all_to_all(v, ('grp', 'row'), 0, 0, axis_index_groups=groups, tiled=T...]
    unnamed x12 -> x4, local copies, waits for them, and re-layouts: 4.8 us -> 0.01 us
    ppermute x2, starting transfers between devices: 9.67 us -> 7.53 us  [other_core(): return lax.ppermute(v, 'grp', [(i, i ^ 1) for i in range(8)])]
where the time goes in v1:
time: 121 us
  blocking collectives  68.1 us (56%)
  Pallas kernels  38.2 us (32%)
  starting transfers between devices  7.53 us (6%)
  waiting for transfers between devices  5.51 us (5%)
    all_to_all x2, blocking collectives, over_near(): lax.all_to_all(v, ('grp', 'row'), 0, 0, axis_index_groups=groups, tiled=T...  53.3 us
    pallas_call x1, Pallas kernels, finished(): pl.pallas_call(body, out_shape=[shape(N, N), shape(N, NRHS), shape(ROWS_D...  24.9 us
    all_to_all x1, blocking collectives, over_far(): return lax.all_to_all(v, 'row', 0, 0, axis_index_groups=groups, tiled=True)  14.9 us
    pallas_call x1, Pallas kernels, terms(): pl.pallas_call(terms_body, out_shape=[shape(UNITS, TALL, NB)] * 2, grid=(...  12.2 us
    ppermute x2, starting transfers between devices, other_core(): return lax.ppermute(v, 'grp', [(i, i ^ 1) for i in range(8)])  7.53 us
    ppermute x2, waiting for transfers between devices, other_core(): return lax.ppermute(v, 'grp', [(i, i ^ 1) for i in range(8)])  5.51 us
  transfers between devices with their start and end apart: 2, of which 2 were waited for; matrix products, arithmetic and copies ran while one was open for 0% of the time, Pallas kernels for 0%

profile of v1, /device:TPU:1, one launch (start us, length us, event | category | flops | bytes accessed | tf_op | source)
XLA Modules:
  0.0 120.7 jit_solution(14177817979611354003)
XLA Ops:
  0.6 12.2 %terms.1 = (f32[128,24,128]{2,1,0:T(8,128)S(1)}, f32[128,24,128]{2,1,0:T(8,128)S(1)}) custom-call(f32[2048,512]{1,0:T(8,128)} %refs_2_.1, f32[2048,128]{1,0:T(8,128)} %refs_3_.1, s32[16,128]{1,0:T(8,128)} %bitcast.5, s32[1,1024]{1,0:T(1,128)} %pick_ref.1), custom_call_target="tpu_custom_call" | custom-call | tf_op jit(solution)/shard_map/terms/pallas_call | solution.py:116
  12.8 3.3 %collective-permute-start = (f32[128,24,128]{2,1,0:T(8,128)S(1)}, f32[128,24,128]{2,1,0:T(8,128)S(1)}, u32[]{:S(2)}, u32[]{:S(2)}) collective-permute-start(f32[128,24,128]{2,1,0:T(8,128)S(1)} %get-tuple-element.6), channel_id=1, source_target_pairs={{0,32},{32,0},{64,96},{96,64},{128,160},{160,128},{192,224},{224,1... | collective-permute-start | bytes 4718600 | tf_op jit(solution)/shard_map/ppermute | solution.py:140
  16.1 3.0 %collective-permute-done = f32[128,24,128]{2,1,0:T(8,128)S(1)} collective-permute-done((f32[128,24,128]{2,1,0:T(8,128)S(1)}, f32[128,24,128]{2,1,0:T(8,128)S(1)}, u32[]{:S(2)}, u32[]{:S(2)}) %collective-permute-start) | collective-permute-done | bytes 1572896 | tf_op jit(solution)/shard_map/ppermute | solution.py:140
  19.1 0.2 add.3
  19.4 29.1 %all_to_all.15 = f32[32,4,24,128]{3,2,1,0:T(8,128)S(1)} all-to-all(f32[32,4,24,128]{3,2,1,0:T(8,128)S(1)} %bitcast.4), channel_id=1, replica_groups={{0,1,8,9,16,17,24,25,64,65,72,73,80,81,88,89,128,129,136,137,144,145,15..., dimensions={0} | all-to-all | bytes 3145728 | tf_op jit(solution)/shard_map/all_to_all | solution.py:153
  48.5 0.1 reduce_sum.18
  48.6 14.9 %all_to_all.16 = f32[4,4,24,128]{3,2,1,0:T(8,128)S(1)} all-to-all(f32[4,4,24,128]{3,2,1,0:T(8,128)S(1)} %broadcast_in_dim.6), channel_id=1, replica_groups={{0,2,4,6},{1,3,5,7},{8,10,12,14},{9,11,13,15},{16,18,20,22},{17,19,21,2..., dimensions={0} | all-to-all | bytes 393216 | tf_op jit(solution)/shard_map/all_to_all | solution.py:158
  63.5 0.2 broadcast_in_dim.7
  63.7 0.0 copy-start
  63.7 24.2 %all_to_all.17 = f32[32,4,24,128]{3,2,1,0:T(8,128)S(1)} all-to-all(f32[32,4,24,128]{3,2,1,0:T(8,128)S(1)} %broadcast_in_dim.7), channel_id=1, replica_groups={{0,1,8,9,16,17,24,25,64,65,72,73,80,81,88,89,128,129,136,137,144,145,15..., dimensions={0} | all-to-all | bytes 3145728 | tf_op jit(solution)/shard_map/all_to_all | solution.py:153
  87.8 0.0 copy-start.1
  87.8 1.0 gram.1.refs_0_
  88.9 4.2 %collective-permute-start.1 = (f32[2304,128]{1,0:T(8,128)S(1)}, f32[2304,128]{1,0:T(8,128)S(1)}, u32[]{:S(2)}, u32[]{:S(2)}) collective-permute-start(f32[2304,128]{1,0:T(8,128)S(1)} %gram.1.refs_0_), channel_id=1, source_target_pairs={{0,32},{32,0},{64,96},{96,64},{128,160},{160,128},{192,224},{224,1... | collective-permute-start | bytes 3538952 | tf_op jit(solution)/shard_map/ppermute | solution.py:140
  93.1 2.5 %collective-permute-done.1.refs_1_ = f32[2304,128]{1,0:T(8,128)S(1)} collective-permute-done((f32[2304,128]{1,0:T(8,128)S(1)}, f32[2304,128]{1,0:T(8,128)S(1)}, u32[]{:S(2)}, u32[]{:S(2)}) %collective-permute-start.1) | collective-permute-done | bytes 1179680 | tf_op jit(solution)/shard_map/ppermute | solution.py:140
  95.6 0.0 copy-done
  95.6 0.0 copy-done.1
  95.6 24.9 %finish.1 = (f32[512,512]{1,0:T(8,128)}, f32[512,128]{1,0:T(8,128)}, f32[2048,128]{1,0:T(8,128)}) custom-call(f32[2304,128]{1,0:T(8,128)S(1)} %gram.1.refs_0_, f32[2304,128]{1,0:T(8,128)S(1)} %collective-permute-done.1.refs_1_, f32[2048,512]{1,0:T(8,128)S(1)} %copy-done, f32[2048,128]{1,0:T(8,128)S(1)} %copy-done.1), custom_call_target="tpu_custom_call" | custom-call | tf_op jit(solution)/shard_map/finish/pallas_call | solution.py:349
  (2 shorter events, 0.0 us)
Async XLA Ops:
  12.8 6.3 %collective-permute-start = (f32[128,24,128]{2,1,0:T(8,128)S(1)}, f32[128,24,128]{2,1,0:T(8,128)S(1)}, u32[]{:S(2)}, u32[]{:S(2)}) collective-permute-start(f32[128,24,128]{2,1,0:T(8,128)S(1)} %get-tuple-element.6), channel_id=1, source_target_pairs={{0,32},{32,0},{64,96},{96,64},{128,160},{160,128},{192,224},{224,1... | collective-permute-start | bytes 4718600 | tf_op jit(solution)/shard_map/ppermute | solution.py:140
  63.7 31.9 %copy-start = (f32[2048,512]{1,0:T(8,128)S(1)}, f32[2048,512]{1,0:T(8,128)}, u32[]{:S(2)}) copy-start(f32[2048,512]{1,0:T(8,128)} %refs_2_.1) | copy-start | bytes 12582916
  87.8 7.8 %copy-start.1 = (f32[2048,128]{1,0:T(8,128)S(1)}, f32[2048,128]{1,0:T(8,128)}, u32[]{:S(2)}) copy-start(f32[2048,128]{1,0:T(8,128)} %refs_3_.1) | copy-start | bytes 3145732
  88.9 6.7 %collective-permute-start.1 = (f32[2304,128]{1,0:T(8,128)S(1)}, f32[2304,128]{1,0:T(8,128)S(1)}, u32[]{:S(2)}, u32[]{:S(2)}) collective-permute-start(f32[2304,128]{1,0:T(8,128)S(1)} %gram.1.refs_0_), channel_id=1, source_target_pairs={{0,32},{32,0},{64,96},{96,64},{128,160},{160,128},{192,224},{224,1... | collective-permute-start | bytes 3538952 | tf_op jit(solution)/shard_map/ppermute | solution.py:140

commit v2 on v1

--- a/solution.py
+++ b/solution.py
@@ -204,7 +204,13 @@
     return jnp.broadcast_to(v[:, j : j + 1], (8, NB))
 
 
-def factor_block(d_ref, b_ref, u_ref, w_ref):
+def tree(vs):
+    while len(vs) > 1:
+        vs = [vs[i] + vs[i + 1] for i in range(0, len(vs) - 1, 2)] + ([vs[-1]] if len(vs) % 2 else [])
+    return vs[0]
+
+
+def factor_block(block, u_ref, w_ref):
     lane = lax.broadcasted_iota(jnp.int32, (8, NB), 1)
     sub = lax.broadcasted_iota(jnp.int32, (8, NB), 0)
 
@@ -214,11 +220,21 @@
             v = jnp.where(sub == m, vs[m], v)
         return v
 
-    for p in range(NB // 8):
+    tiles = list(block)
+    last = NB // 8 - 1
+    cols = [lanes_of(tiles[0], m) for m in range(8)]
+    for p in range(last + 1):
         q = 8 * p
-        cols = [lanes_of(d_ref[q : q + 8, :], q + m) for m in range(8)]
+        t = tiles[p]
         s = {(k, m): rows_of(cols[m], k) for m in range(8) for k in range(m, 8)}
-        l, r = {}, {}
+        inside = (lane >= q) & (lane < q + 8)
+        own = jnp.where(inside, jnp.where(lane == q + sub, 1.0, 0.0), t)
+        own = [rows_of(own, m) for m in range(8)]
+        close = [i for i in (p + 1, p + 2) if i <= last]
+        near = {i: [lanes_of(tiles[i], q + m) for m in range(8)] for i in close}
+        ahead = [lanes_of(tiles[p + 1], q + 8 + m) for m in range(8)] if close else None
+        l, r, u = {}, {}, []
+        c = {i: [] for i in close}
         for m in range(8):
             r[m] = lax.rsqrt(s[m, m])
             for k in range(m + 1, 8):
@@ -226,77 +242,78 @@
             for k in range(m + 1, 8):
                 for j in range(m + 1, k + 1):
                     s[k, j] = s[k, j] - l[k, m] * l[j, m]
-
-        def forward(vs):
-            out = []
-            for m in range(8):
-                v = vs[m]
-                for k in range(m):
-                    v = v - l[m, k] * out[k]
-                out.append(v * r[m])
-            return out
-
-        t, tb = d_ref[q : q + 8, :], b_ref[q : q + 8, :]
-        u = forward([rows_of(t, m) for m in range(8)])
-        w = forward([rows_of(tb, m) for m in range(8)])
-        u_ref[q : q + 8, :] = jnp.where(lane >= q + sub, packed(u), 0.0)
-        w_ref[q : q + 8, :] = packed(w)
-        for i in range(p + 1, NB // 8):
-            o = 8 * i
-            v, y = d_ref[o : o + 8, :], b_ref[o : o + 8, :]
-            c = forward([lanes_of(v, q + m) for m in range(8)])
-            for m in range(8):
-                v = v - c[m] * u[m]
-                y = y - c[m] * w[m]
-            d_ref[o : o + 8, :] = v
-            b_ref[o : o + 8, :] = y
+            for i in close:
+                c[i].append(near[i][m] * r[m])
+                for k in range(m + 1, 8):
+                    near[i][k] = near[i][k] - l[k, m] * c[i][m]
+            if close:
+                ahead = [ahead[n] - c[p + 1][m] * rows_of(c[p + 1][m], n) for n in range(8)]
+            u.append(own[m] * r[m])
+            for k in range(m + 1, 8):
+                own[k] = own[k] - l[k, m] * u[m]
+        for i in close:
+            cleared = jnp.where(inside, 0.0, tiles[i])
+            tiles[i] = cleared - tree([c[i][m] * u[m] for m in range(8)])
+        cols = ahead
+        flat = packed(u)
+        w_ref[q : q + 8, :] = jnp.where(lane < q + 8, flat, 0.0)
+        diag = jnp.where(lane >= q + 8, flat, 0.0)
+        for m in range(8):
+            diag = jnp.where((lane == q + m) & (sub == m), r[m] * s[m, m], diag)
+            for k in range(m + 1, 8):
+                diag = jnp.where((lane == q + k) & (sub == m), l[k, m], diag)
+        u_ref[q : q + 8, :] = diag
+        if p + 3 <= last:
+            z = [None] * 8
+            for m in range(7, -1, -1):
+                v = u[m]
+                for k in range(m + 1, 8):
+                    v = v - l[k, m] * z[k]
+                z[m] = v * r[m]
+            for i in range(p + 3, last + 1):
+                v = tiles[i]
+                cleared = jnp.where(inside, 0.0, v)
+                tiles[i] = cleared - tree([lanes_of(v, q + m) * z[m] for m in range(8)])
 
 
 def finish_body(
-    gram_scale, grad_scale, own_ref, got_ref, a_hbm, t_hbm, l_ref, x_ref, r_hbm,
-    a_ref, b_ref, d_ref, db_ref, w_ref, u_ref, lt_ref, li_ref, m_ref, mat_ref, t_ref, r_ref, sems,
+    gram_scale, grad_scale, own_ref, got_ref, mat_ref, t_ref, l_ref, x_ref, r_hbm,
+    a_ref, b_ref, lt_ref, li_ref, m_ref, r_ref, sems,
 ):
-    fetch = [pltpu.make_async_copy(a_hbm, mat_ref, sems.at[0]), pltpu.make_async_copy(t_hbm, t_ref, sems.at[1])]
-    for copy in fetch:
-        copy.start()
-    zeros = jnp.zeros((NB, NB), F32)
     for b, (i, j) in enumerate(LOWER):
         rows = slice(b * NB, (b + 1) * NB)
         g = (own_ref[rows, :] + got_ref[rows, :]) * gram_scale
-        a_ref[i * NB : (i + 1) * NB, j * NB : (j + 1) * NB] = g
+        a_ref[j * NB : (j + 1) * NB, i * NB : (i + 1) * NB] = g.T if i != j else g
+    for i, j in LOWER:
         if i != j:
-            a_ref[j * NB : (j + 1) * NB, i * NB : (i + 1) * NB] = g.T
-    lt_ref[...] = jnp.zeros_like(lt_ref)
-    li_ref[...] = jnp.zeros_like(li_ref)
-    b_ref[...] = jnp.zeros_like(b_ref)
-    row = lax.broadcasted_iota(jnp.int32, (NB, NB), 0)
-    eye = (row == lax.broadcasted_iota(jnp.int32, (NB, NB), 1)).astype(F32)
-
-    def block(step, _):
-        here = pl.ds(pl.multiple_of(step * NB, NB), NB)
-        d_ref[...] = a_ref[here, here]
-        db_ref[...] = eye
-        factor_block(d_ref, db_ref, u_ref, w_ref)
-        lt_ref[here, here] = u_ref[...]
-        li_ref[here, here] = w_ref[...]
-        for j in range(N // NB):
-
-            @pl.when(step == j)
-            def _(j=j):
-                o, e = j * NB, (j + 1) * NB
-                w = w_ref[...]
-                if j:
-                    li_ref[o:e, 0:o] = dot_hi(w, b_ref[o:e, 0:o])
-                if e < N:
-                    u = dot_hi(w, a_ref[o:e, e:])
-                    lt_ref[o:e, e:] = u
-                    ut = u.T
-                    a_ref[e:, e:] = a_ref[e:, e:] - dot_hi(ut, u)
-                    b_ref[e:, 0:e] = b_ref[e:, 0:e] - dot_hi(ut, li_ref[o:e, 0:e])
-
-        return 0
-
-    lax.fori_loop(0, N // NB, block, 0)
+            zeros = jnp.zeros((NB, NB), F32)
+            lt_ref[i * NB : (i + 1) * NB, j * NB : (j + 1) * NB] = zeros
+            li_ref[j * NB : (j + 1) * NB, i * NB : (i + 1) * NB] = zeros
+    for j in range(N // NB):
+        o, e, f = j * NB, (j + 1) * NB, (j + 2) * NB
+        tiles = [a_ref[o + 8 * i : o + 8 * i + 8, o:e] for i in range(NB // 8)]
+        factor_block(tiles, lt_ref.at[o:e, o:e], li_ref.at[o:e, o:e])
+        w = li_ref[o:e, o:e]
+        if e < N:
+            u = dot_hi(w, a_ref[o:e, e:f])
+            ut = u.T
+            lt_ref[o:e, e:f] = u
+            a_ref[e:f, e:f] = a_ref[e:f, e:f] - dot_hi(ut, u)
+        if j:
+            li_ref[o:e, 0:o] = dot_hi(w, b_ref[o:e, 0:o])
+        if f < N:
+            rest = dot_hi(w, a_ref[o:e, f:])
+            lt_ref[o:e, f:] = rest
+            a_ref[e:f, f:] = a_ref[e:f, f:] - dot_hi(ut, rest)
+            for g in range(f, N, NB):
+                h = g + NB
+                a_ref[g:h, g:] = a_ref[g:h, g:] - dot_hi(lt_ref[o:e, g:h].T, lt_ref[o:e, g:])
+        for g in range(e, N, NB):
+            h = g + NB
+            new = dot_hi(ut if g == e else lt_ref[o:e, g:h].T, li_ref[o:e, 0:e])
+            if j:
+                b_ref[g:h, 0:o] = b_ref[g:h, 0:o] - new[:, :o]
+            b_ref[g:h, o:e] = -new[:, o:]
     l_ref[...] = lt_ref[...].T
 
     base = len(LOWER) * NB
@@ -325,8 +342,6 @@
     for _ in range(ITERS - 1):
         x = x + times(turned, times(inverse, first - times(moments, x)))
     x_ref[...] = x
-    for copy in fetch:
-        copy.wait()
     xs = jnp.concatenate(split(x), axis=1)
     puts = []
     deep = ROWS_DEV // 4
@@ -335,7 +350,7 @@
         hi, lo = split(mat_ref[rows, :])
         ahead, behind = dot(hi, xs), dot(lo, xs)
         r_ref[rows, :] = t_ref[rows, :] - (ahead[:, :NRHS] + ((ahead[:, NRHS:] + behind[:, :NRHS]) + behind[:, NRHS:]))
-        puts.append(pltpu.make_async_copy(r_ref.at[rows, :], r_hbm.at[rows, :], sems.at[2 + c]))
+        puts.append(pltpu.make_async_copy(r_ref.at[rows, :], r_hbm.at[rows, :], sems.at[c]))
         puts[-1].start()
     for copy in puts:
         copy.wait()
@@ -349,15 +364,10 @@
     return pl.pallas_call(
         body,
         out_shape=[shape(N, N), shape(N, NRHS), shape(ROWS_DEV, NRHS)],
-        in_specs=[vmem, vmem, hbm, hbm],
+        in_specs=[vmem] * 4,
         out_specs=[vmem, vmem, hbm],
-        scratch_shapes=[V((N, N), F32)] * 2
-        + [V((NB, NB), F32)] * 4
-        + [V((N, N), F32)] * 3
-        + [V((ROWS_DEV, N), F32)]
-        + [V((ROWS_DEV, NRHS), F32)] * 2
-        + [pltpu.SemaphoreType.DMA((6,))],
-        compiler_params=pltpu.CompilerParams(vmem_limit_bytes=40 * MIB),
+        scratch_shapes=[V((N, N), F32)] * 5 + [V((ROWS_DEV, NRHS), F32), pltpu.SemaphoreType.DMA((4,))],
+        compiler_params=pltpu.CompilerParams(vmem_limit_bytes=32 * MIB),
         name="finish",
     )(own, got, matrix, targets)
 

time: 121 us -> 115 us (0.950)
  Pallas kernels: 38.2 us -> 32.1 us
    pallas_call x1, Pallas kernels: 24.9 us -> 18.9 us  [finished(): pl.pallas_call(body, out_shape=[shape(N, N), shape(N, NRHS), shape(ROWS_D...]
where the time goes in v2:
time: 115 us
  blocking collectives  68.1 us (59%)
  Pallas kernels  32.1 us (28%)
  starting transfers between devices  7.53 us (7%)
  waiting for transfers between devices  5.51 us (5%)
    all_to_all x2, blocking collectives, over_near(): lax.all_to_all(v, ('grp', 'row'), 0, 0, axis_index_groups=groups, tiled=T...  53.3 us
    pallas_call x1, Pallas kernels, finished(): pl.pallas_call(body, out_shape=[shape(N, N), shape(N, NRHS), shape(ROWS_D...  18.9 us
    all_to_all x1, blocking collectives, over_far(): return lax.all_to_all(v, 'row', 0, 0, axis_index_groups=groups, tiled=True)  14.9 us
    pallas_call x1, Pallas kernels, terms(): pl.pallas_call(terms_body, out_shape=[shape(UNITS, TALL, NB)] * 2, grid=(...  12.2 us
    ppermute x2, starting transfers between devices, other_core(): return lax.ppermute(v, 'grp', [(i, i ^ 1) for i in range(8)])  7.53 us
    ppermute x2, waiting for transfers between devices, other_core(): return lax.ppermute(v, 'grp', [(i, i ^ 1) for i in range(8)])  5.51 us
  transfers between devices with their start and end apart: 2, of which 2 were waited for; matrix products, arithmetic and copies ran while one was open for 0% of the time, Pallas kernels for 0%

profile of v2, /device:TPU:1, one launch (start us, length us, event | category | flops | bytes accessed | tf_op | source)
XLA Modules:
  0.0 114.7 jit_solution(10513817780429628466)
XLA Ops:
  0.6 12.2 %terms.1 = (f32[128,24,128]{2,1,0:T(8,128)S(1)}, f32[128,24,128]{2,1,0:T(8,128)S(1)}) custom-call(f32[2048,512]{1,0:T(8,128)} %refs_2_.1, f32[2048,128]{1,0:T(8,128)} %refs_3_.1, s32[16,128]{1,0:T(8,128)} %bitcast.5, s32[1,1024]{1,0:T(1,128)} %pick_ref.1), custom_call_target="tpu_custom_call" | custom-call | tf_op jit(solution)/shard_map/terms/pallas_call | solution.py:116
  12.8 3.3 %collective-permute-start = (f32[128,24,128]{2,1,0:T(8,128)S(1)}, f32[128,24,128]{2,1,0:T(8,128)S(1)}, u32[]{:S(2)}, u32[]{:S(2)}) collective-permute-start(f32[128,24,128]{2,1,0:T(8,128)S(1)} %get-tuple-element.6), channel_id=1, source_target_pairs={{0,32},{32,0},{64,96},{96,64},{128,160},{160,128},{192,224},{224,1... | collective-permute-start | bytes 4718600 | tf_op jit(solution)/shard_map/ppermute | solution.py:140
  16.1 3.0 %collective-permute-done = f32[128,24,128]{2,1,0:T(8,128)S(1)} collective-permute-done((f32[128,24,128]{2,1,0:T(8,128)S(1)}, f32[128,24,128]{2,1,0:T(8,128)S(1)}, u32[]{:S(2)}, u32[]{:S(2)}) %collective-permute-start) | collective-permute-done | bytes 1572896 | tf_op jit(solution)/shard_map/ppermute | solution.py:140
  19.1 0.2 add.3
  19.4 29.1 %all_to_all.15 = f32[32,4,24,128]{3,2,1,0:T(8,128)S(1)} all-to-all(f32[32,4,24,128]{3,2,1,0:T(8,128)S(1)} %bitcast.4), channel_id=1, replica_groups={{0,1,8,9,16,17,24,25,64,65,72,73,80,81,88,89,128,129,136,137,144,145,15..., dimensions={0} | all-to-all | bytes 3145728 | tf_op jit(solution)/shard_map/all_to_all | solution.py:153
  48.5 0.1 reduce_sum.18
  48.6 14.9 %all_to_all.16 = f32[4,4,24,128]{3,2,1,0:T(8,128)S(1)} all-to-all(f32[4,4,24,128]{3,2,1,0:T(8,128)S(1)} %broadcast_in_dim.6), channel_id=1, replica_groups={{0,2,4,6},{1,3,5,7},{8,10,12,14},{9,11,13,15},{16,18,20,22},{17,19,21,2..., dimensions={0} | all-to-all | bytes 393216 | tf_op jit(solution)/shard_map/all_to_all | solution.py:158
  63.5 0.2 broadcast_in_dim.7
  63.7 0.0 copy-start
  63.7 24.2 %all_to_all.17 = f32[32,4,24,128]{3,2,1,0:T(8,128)S(1)} all-to-all(f32[32,4,24,128]{3,2,1,0:T(8,128)S(1)} %broadcast_in_dim.7), channel_id=1, replica_groups={{0,1,8,9,16,17,24,25,64,65,72,73,80,81,88,89,128,129,136,137,144,145,15..., dimensions={0} | all-to-all | bytes 3145728 | tf_op jit(solution)/shard_map/all_to_all | solution.py:153
  87.8 0.0 copy-start.1
  87.8 1.0 gram.1.refs_0_
  88.9 4.2 %collective-permute-start.1 = (f32[2304,128]{1,0:T(8,128)S(1)}, f32[2304,128]{1,0:T(8,128)S(1)}, u32[]{:S(2)}, u32[]{:S(2)}) collective-permute-start(f32[2304,128]{1,0:T(8,128)S(1)} %gram.1.refs_0_), channel_id=1, source_target_pairs={{0,32},{32,0},{64,96},{96,64},{128,160},{160,128},{192,224},{224,1... | collective-permute-start | bytes 3538952 | tf_op jit(solution)/shard_map/ppermute | solution.py:140
  93.1 2.5 %collective-permute-done.1.refs_1_ = f32[2304,128]{1,0:T(8,128)S(1)} collective-permute-done((f32[2304,128]{1,0:T(8,128)S(1)}, f32[2304,128]{1,0:T(8,128)S(1)}, u32[]{:S(2)}, u32[]{:S(2)}) %collective-permute-start.1) | collective-permute-done | bytes 1179680 | tf_op jit(solution)/shard_map/ppermute | solution.py:140
  95.6 0.0 copy-done
  95.6 0.0 copy-done.1
  95.6 18.9 %finish.1 = (f32[512,512]{1,0:T(8,128)}, f32[512,128]{1,0:T(8,128)}, f32[2048,128]{1,0:T(8,128)}) custom-call(f32[2304,128]{1,0:T(8,128)S(1)} %gram.1.refs_0_, f32[2304,128]{1,0:T(8,128)S(1)} %collective-permute-done.1.refs_1_, f32[2048,512]{1,0:T(8,128)S(1)} %copy-done, f32[2048,128]{1,0:T(8,128)S(1)} %copy-done.1), custom_call_target="tpu_custom_call" | custom-call | tf_op jit(solution)/shard_map/finish/pallas_call | solution.py:364
  (2 shorter events, 0.0 us)
Async XLA Ops:
  12.8 6.3 %collective-permute-start = (f32[128,24,128]{2,1,0:T(8,128)S(1)}, f32[128,24,128]{2,1,0:T(8,128)S(1)}, u32[]{:S(2)}, u32[]{:S(2)}) collective-permute-start(f32[128,24,128]{2,1,0:T(8,128)S(1)} %get-tuple-element.6), channel_id=1, source_target_pairs={{0,32},{32,0},{64,96},{96,64},{128,160},{160,128},{192,224},{224,1... | collective-permute-start | bytes 4718600 | tf_op jit(solution)/shard_map/ppermute | solution.py:140
  63.7 31.9 %copy-start = (f32[2048,512]{1,0:T(8,128)S(1)}, f32[2048,512]{1,0:T(8,128)}, u32[]{:S(2)}) copy-start(f32[2048,512]{1,0:T(8,128)} %refs_2_.1) | copy-start | bytes 12582916
  87.8 7.8 %copy-start.1 = (f32[2048,128]{1,0:T(8,128)S(1)}, f32[2048,128]{1,0:T(8,128)}, u32[]{:S(2)}) copy-start(f32[2048,128]{1,0:T(8,128)} %refs_3_.1) | copy-start | bytes 3145732
  88.9 6.7 %collective-permute-start.1 = (f32[2304,128]{1,0:T(8,128)S(1)}, f32[2304,128]{1,0:T(8,128)S(1)}, u32[]{:S(2)}, u32[]{:S(2)}) collective-permute-start(f32[2304,128]{1,0:T(8,128)S(1)} %gram.1.refs_0_), channel_id=1, source_target_pairs={{0,32},{32,0},{64,96},{96,64},{128,160},{160,128},{192,224},{224,1... | collective-permute-start | bytes 3538952 | tf_op jit(solution)/shard_map/ppermute | solution.py:140

commit v3 on v2

--- a/solution.py
+++ b/solution.py
@@ -53,7 +53,7 @@
     return v & 1
 
 
-def terms_body(a_ref, t_ref, sign_ref, pick_ref, keep_ref, send_ref, base_ref, high_ref, acc_ref, nacc_ref, p_ref):
+def terms_body(a_ref, t_ref, sign_ref, pick_ref, keep_ref, send_ref, base_ref, high_ref, h_ref, acc_ref, nacc_ref, p_ref):
     k = pl.program_id(0)
     depth = a_ref.shape[0]
 
@@ -76,15 +76,19 @@
         rows = slice(b * NB, (b + 1) * NB)
         turn = (1 - 2 * parity(high_ref[rows, :] & k, 4)).astype(F32)
         turn = jnp.concatenate([turn] * (depth // NB), axis=1) * flips
-        h = base_ref[rows, :] * turn.astype(BF16)
-        acc_ref[rows, :] += dot(h, hi) + dot(h, lo)
+        h_ref[rows, :] = base_ref[rows, :] * turn.astype(BF16)
+    h = jnp.concatenate([h_ref[...]] * 2, axis=1)
+    both = jnp.concatenate([hi, lo], axis=0)
+    for c in (0, N // 2):
+        acc_ref[:, c : c + N // 2] += dot(h, both[:, c : c + N // 2])
 
     thi, tlo = split(t_ref[...])
     his, los = jnp.concatenate([thi, hi], axis=1), jnp.concatenate([tlo, lo], axis=1)
+    right = jnp.concatenate([his, los, his], axis=0)
     hit, lot = hi.T, lo.T
-    for i in range(4):
-        rows, wide = slice(i * NB, (i + 1) * NB), (i + 2) * NB
-        nacc_ref[rows, :wide] += dot(hit[rows], his[:, :wide]) + (dot(hit[rows], los[:, :wide]) + dot(lot[rows], his[:, :wide]))
+    left = jnp.concatenate([hit, hit, lot], axis=1)
+    for top, c, e in ((0, 0, 2 * NB), (NB, 2 * NB, 4 * NB), (3 * NB, 4 * NB, 5 * NB)):
+        nacc_ref[top:, c:e] += dot(left[top:], right[:, c:e])
 
     @pl.when(k == pl.num_programs(0) - 1)
     def _():
@@ -127,6 +131,7 @@
         scratch_shapes=[
             V((SK, depth), BF16),
             V((SK, NB), jnp.int32),
+            V((SK, depth), BF16),
             V((SK, N), F32),
             V((N, N + NRHS), F32),
             V((2, 8, NB, NB), F32),
@@ -210,7 +215,7 @@
     return vs[0]
 
 
-def factor_block(block, u_ref, w_ref):
+def factor_block(block, u_ref, d_ref, w_ref):
     lane = lax.broadcasted_iota(jnp.int32, (8, NB), 1)
     sub = lax.broadcasted_iota(jnp.int32, (8, NB), 0)
 
@@ -226,7 +231,6 @@
     for p in range(last + 1):
         q = 8 * p
         t = tiles[p]
-        s = {(k, m): rows_of(cols[m], k) for m in range(8) for k in range(m, 8)}
         inside = (lane >= q) & (lane < q + 8)
         own = jnp.where(inside, jnp.where(lane == q + sub, 1.0, 0.0), t)
         own = [rows_of(own, m) for m in range(8)]
@@ -235,13 +239,15 @@
         ahead = [lanes_of(tiles[p + 1], q + 8 + m) for m in range(8)] if close else None
         l, r, u = {}, {}, []
         c = {i: [] for i in close}
+        diag = jnp.zeros((8, NB), F32)
         for m in range(8):
-            r[m] = lax.rsqrt(s[m, m])
+            pivot = rows_of(cols[m], m)
+            r[m] = lax.rsqrt(pivot)
+            low = cols[m] * r[m]
+            diag = jnp.where(lane == q + m, low, diag)
             for k in range(m + 1, 8):
-                l[k, m] = s[k, m] * r[m]
-            for k in range(m + 1, 8):
-                for j in range(m + 1, k + 1):
-                    s[k, j] = s[k, j] - l[k, m] * l[j, m]
+                l[k, m] = rows_of(low, k)
+                cols[k] = cols[k] - low * l[k, m]
             for i in close:
                 c[i].append(near[i][m] * r[m])
                 for k in range(m + 1, 8):
@@ -257,12 +263,8 @@
         cols = ahead
         flat = packed(u)
         w_ref[q : q + 8, :] = jnp.where(lane < q + 8, flat, 0.0)
-        diag = jnp.where(lane >= q + 8, flat, 0.0)
-        for m in range(8):
-            diag = jnp.where((lane == q + m) & (sub == m), r[m] * s[m, m], diag)
-            for k in range(m + 1, 8):
-                diag = jnp.where((lane == q + k) & (sub == m), l[k, m], diag)
-        u_ref[q : q + 8, :] = diag
+        u_ref[q : q + 8, :] = jnp.where(lane >= q + 8, flat, 0.0)
+        d_ref[q : q + 8, :] = jnp.where(q + sub >= lane, diag, 0.0)
         if p + 3 <= last:
             z = [None] * 8
             for m in range(7, -1, -1):
@@ -278,7 +280,7 @@
 
 def finish_body(
     gram_scale, grad_scale, own_ref, got_ref, mat_ref, t_ref, l_ref, x_ref, r_hbm,
-    a_ref, b_ref, lt_ref, li_ref, m_ref, r_ref, sems,
+    a_ref, b_ref, lt_ref, li_ref, m_ref, d_ref, r_ref, sems,
 ):
     for b, (i, j) in enumerate(LOWER):
         rows = slice(b * NB, (b + 1) * NB)
@@ -292,7 +294,7 @@
     for j in range(N // NB):
         o, e, f = j * NB, (j + 1) * NB, (j + 2) * NB
         tiles = [a_ref[o + 8 * i : o + 8 * i + 8, o:e] for i in range(NB // 8)]
-        factor_block(tiles, lt_ref.at[o:e, o:e], li_ref.at[o:e, o:e])
+        factor_block(tiles, lt_ref.at[o:e, o:e], d_ref.at[o:e, :], li_ref.at[o:e, o:e])
         w = li_ref[o:e, o:e]
         if e < N:
             u = dot_hi(w, a_ref[o:e, e:f])
@@ -315,6 +317,9 @@
                 b_ref[g:h, 0:o] = b_ref[g:h, 0:o] - new[:, :o]
             b_ref[g:h, o:e] = -new[:, o:]
     l_ref[...] = lt_ref[...].T
+    for o in range(0, N, NB):
+        e = o + NB
+        l_ref[o:e, o:e] = lt_ref[o:e, o:e].T + d_ref[o:e, :]
 
     base = len(LOWER) * NB
 
@@ -366,7 +371,7 @@
         out_shape=[shape(N, N), shape(N, NRHS), shape(ROWS_DEV, NRHS)],
         in_specs=[vmem] * 4,
         out_specs=[vmem, vmem, hbm],
-        scratch_shapes=[V((N, N), F32)] * 5 + [V((ROWS_DEV, NRHS), F32), pltpu.SemaphoreType.DMA((4,))],
+        scratch_shapes=[V((N, N), F32)] * 5 + [V((N, NB), F32), V((ROWS_DEV, NRHS), F32), pltpu.SemaphoreType.DMA((4,))],
         compiler_params=pltpu.CompilerParams(vmem_limit_bytes=32 * MIB),
         name="finish",
     )(own, got, matrix, targets)

time: 115 us -> 114 us (level)
  no operation moved by 1% of the time
where the time goes in v3:
time: 114 us
  blocking collectives  68.1 us (60%)
  Pallas kernels  31.7 us (28%)
  starting transfers between devices  7.52 us (7%)
  waiting for transfers between devices  5.51 us (5%)
    all_to_all x2, blocking collectives, over_near(): lax.all_to_all(v, ('grp', 'row'), 0, 0, axis_index_groups=groups, tiled=T...  53.3 us
    pallas_call x1, Pallas kernels, finished(): pl.pallas_call(body, out_shape=[shape(N, N), shape(N, NRHS), shape(ROWS_D...  18.6 us
    all_to_all x1, blocking collectives, over_far(): return lax.all_to_all(v, 'row', 0, 0, axis_index_groups=groups, tiled=True)  14.9 us
    pallas_call x1, Pallas kernels, terms(): pl.pallas_call(terms_body, out_shape=[shape(UNITS, TALL, NB)] * 2, grid=(...  12 us
    ppermute x2, starting transfers between devices, other_core(): return lax.ppermute(v, 'grp', [(i, i ^ 1) for i in range(8)])  7.52 us
    ppermute x2, waiting for transfers between devices, other_core(): return lax.ppermute(v, 'grp', [(i, i ^ 1) for i in range(8)])  5.51 us
  transfers between devices with their start and end apart: 2, of which 2 were waited for; matrix products, arithmetic and copies ran while one was open for 0% of the time, Pallas kernels for 0%

profile of v3, /device:TPU:1, one launch (start us, length us, event | category | flops | bytes accessed | tf_op | source)
XLA Modules:
  0.0 114.2 jit_solution(10885575196644381386)
XLA Ops:
  0.6 12.0 %terms.1 = (f32[128,24,128]{2,1,0:T(8,128)S(1)}, f32[128,24,128]{2,1,0:T(8,128)S(1)}) custom-call(f32[2048,512]{1,0:T(8,128)} %refs_2_.1, f32[2048,128]{1,0:T(8,128)} %refs_3_.1, s32[16,128]{1,0:T(8,128)} %bitcast.5, s32[1,1024]{1,0:T(1,128)} %pick_ref.1), custom_call_target="tpu_custom_call" | custom-call | tf_op jit(solution)/shard_map/terms/pallas_call | solution.py:120
  12.6 3.3 %collective-permute-start = (f32[128,24,128]{2,1,0:T(8,128)S(1)}, f32[128,24,128]{2,1,0:T(8,128)S(1)}, u32[]{:S(2)}, u32[]{:S(2)}) collective-permute-start(f32[128,24,128]{2,1,0:T(8,128)S(1)} %get-tuple-element.6), channel_id=1, source_target_pairs={{0,32},{32,0},{64,96},{96,64},{128,160},{160,128},{192,224},{224,1... | collective-permute-start | bytes 4718600 | tf_op jit(solution)/shard_map/ppermute | solution.py:145
  15.9 3.0 %collective-permute-done = f32[128,24,128]{2,1,0:T(8,128)S(1)} collective-permute-done((f32[128,24,128]{2,1,0:T(8,128)S(1)}, f32[128,24,128]{2,1,0:T(8,128)S(1)}, u32[]{:S(2)}, u32[]{:S(2)}) %collective-permute-start) | collective-permute-done | bytes 1572896 | tf_op jit(solution)/shard_map/ppermute | solution.py:145
  18.9 0.2 add.3
  19.2 29.1 %all_to_all.15 = f32[32,4,24,128]{3,2,1,0:T(8,128)S(1)} all-to-all(f32[32,4,24,128]{3,2,1,0:T(8,128)S(1)} %bitcast.4), channel_id=1, replica_groups={{0,1,8,9,16,17,24,25,64,65,72,73,80,81,88,89,128,129,136,137,144,145,15..., dimensions={0} | all-to-all | bytes 3145728 | tf_op jit(solution)/shard_map/all_to_all | solution.py:158
  48.3 0.1 reduce_sum.18
  48.4 14.9 %all_to_all.16 = f32[4,4,24,128]{3,2,1,0:T(8,128)S(1)} all-to-all(f32[4,4,24,128]{3,2,1,0:T(8,128)S(1)} %broadcast_in_dim.6), channel_id=1, replica_groups={{0,2,4,6},{1,3,5,7},{8,10,12,14},{9,11,13,15},{16,18,20,22},{17,19,21,2..., dimensions={0} | all-to-all | bytes 393216 | tf_op jit(solution)/shard_map/all_to_all | solution.py:163
  63.3 0.2 broadcast_in_dim.7
  63.5 0.0 copy-start
  63.5 24.2 %all_to_all.17 = f32[32,4,24,128]{3,2,1,0:T(8,128)S(1)} all-to-all(f32[32,4,24,128]{3,2,1,0:T(8,128)S(1)} %broadcast_in_dim.7), channel_id=1, replica_groups={{0,1,8,9,16,17,24,25,64,65,72,73,80,81,88,89,128,129,136,137,144,145,15..., dimensions={0} | all-to-all | bytes 3145728 | tf_op jit(solution)/shard_map/all_to_all | solution.py:158
  87.6 0.0 copy-start.1
  87.6 1.1 gram.1.refs_0_
  88.7 4.2 %collective-permute-start.1 = (f32[2304,128]{1,0:T(8,128)S(1)}, f32[2304,128]{1,0:T(8,128)S(1)}, u32[]{:S(2)}, u32[]{:S(2)}) collective-permute-start(f32[2304,128]{1,0:T(8,128)S(1)} %gram.1.refs_0_), channel_id=1, source_target_pairs={{0,32},{32,0},{64,96},{96,64},{128,160},{160,128},{192,224},{224,1... | collective-permute-start | bytes 3538952 | tf_op jit(solution)/shard_map/ppermute | solution.py:145
  92.9 2.5 %collective-permute-done.1.refs_1_ = f32[2304,128]{1,0:T(8,128)S(1)} collective-permute-done((f32[2304,128]{1,0:T(8,128)S(1)}, f32[2304,128]{1,0:T(8,128)S(1)}, u32[]{:S(2)}, u32[]{:S(2)}) %collective-permute-start.1) | collective-permute-done | bytes 1179680 | tf_op jit(solution)/shard_map/ppermute | solution.py:145
  95.4 0.0 copy-done
  95.4 0.0 copy-done.1
  95.4 18.6 %finish.1 = (f32[512,512]{1,0:T(8,128)}, f32[512,128]{1,0:T(8,128)}, f32[2048,128]{1,0:T(8,128)}) custom-call(f32[2304,128]{1,0:T(8,128)S(1)} %gram.1.refs_0_, f32[2304,128]{1,0:T(8,128)S(1)} %collective-permute-done.1.refs_1_, f32[2048,512]{1,0:T(8,128)S(1)} %copy-done, f32[2048,128]{1,0:T(8,128)S(1)} %copy-done.1), custom_call_target="tpu_custom_call" | custom-call | tf_op jit(solution)/shard_map/finish/pallas_call | solution.py:369
  (2 shorter events, 0.0 us)
Async XLA Ops:
  12.6 6.3 %collective-permute-start = (f32[128,24,128]{2,1,0:T(8,128)S(1)}, f32[128,24,128]{2,1,0:T(8,128)S(1)}, u32[]{:S(2)}, u32[]{:S(2)}) collective-permute-start(f32[128,24,128]{2,1,0:T(8,128)S(1)} %get-tuple-element.6), channel_id=1, source_target_pairs={{0,32},{32,0},{64,96},{96,64},{128,160},{160,128},{192,224},{224,1... | collective-permute-start | bytes 4718600 | tf_op jit(solution)/shard_map/ppermute | solution.py:145
  63.5 31.9 %copy-start = (f32[2048,512]{1,0:T(8,128)S(1)}, f32[2048,512]{1,0:T(8,128)}, u32[]{:S(2)}) copy-start(f32[2048,512]{1,0:T(8,128)} %refs_2_.1) | copy-start | bytes 12582916
  87.6 7.8 %copy-start.1 = (f32[2048,128]{1,0:T(8,128)S(1)}, f32[2048,128]{1,0:T(8,128)}, u32[]{:S(2)}) copy-start(f32[2048,128]{1,0:T(8,128)} %refs_3_.1) | copy-start | bytes 3145732
  88.7 6.7 %collective-permute-start.1 = (f32[2304,128]{1,0:T(8,128)S(1)}, f32[2304,128]{1,0:T(8,128)S(1)}, u32[]{:S(2)}, u32[]{:S(2)}) collective-permute-start(f32[2304,128]{1,0:T(8,128)S(1)} %gram.1.refs_0_), channel_id=1, source_target_pairs={{0,32},{32,0},{64,96},{96,64},{128,160},{160,128},{192,224},{224,1... | collective-permute-start | bytes 3538952 | tf_op jit(solution)/shard_map/ppermute | solution.py:145

commit v4 on v3

--- a/solution.py
+++ b/solution.py
@@ -42,6 +42,11 @@
 
 def dot_hi(a, b, dims=NN):
     return lax.dot_general(a, b, dims, precision=HI, preferred_element_type=F32)
+
+
+def dot_parts(a, b):
+    (ah, al), (bh, bl) = split(a), split(b)
+    return dot(jnp.concatenate([ah, ah, al], axis=1), jnp.concatenate([bh, bl, bh], axis=0))
 
 
 def parity(v, bits):
@@ -302,7 +307,7 @@
             lt_ref[o:e, e:f] = u
             a_ref[e:f, e:f] = a_ref[e:f, e:f] - dot_hi(ut, u)
         if j:
-            li_ref[o:e, 0:o] = dot_hi(w, b_ref[o:e, 0:o])
+            li_ref[o:e, 0:o] = dot_parts(w, b_ref[o:e, 0:o])
         if f < N:
             rest = dot_hi(w, a_ref[o:e, f:])
             lt_ref[o:e, f:] = rest
@@ -312,7 +317,7 @@
                 a_ref[g:h, g:] = a_ref[g:h, g:] - dot_hi(lt_ref[o:e, g:h].T, lt_ref[o:e, g:])
         for g in range(e, N, NB):
             h = g + NB
-            new = dot_hi(ut if g == e else lt_ref[o:e, g:h].T, li_ref[o:e, 0:e])
+            new = dot_parts(ut if g == e else lt_ref[o:e, g:h].T, li_ref[o:e, 0:e])
             if j:
                 b_ref[g:h, 0:o] = b_ref[g:h, 0:o] - new[:, :o]
             b_ref[g:h, o:e] = -new[:, o:]

time: 114 us -> 114 us (level)
  no operation moved by 1% of the time
where the time goes in v4:
time: 114 us
  blocking collectives  68.1 us (60%)
  Pallas kernels  31.1 us (27%)
  starting transfers between devices  7.52 us (7%)
  waiting for transfers between devices  5.51 us (5%)
    all_to_all x2, blocking collectives, over_near(): lax.all_to_all(v, ('grp', 'row'), 0, 0, axis_index_groups=groups, tiled=T...  53.3 us
    pallas_call x1, Pallas kernels, finished(): pl.pallas_call(body, out_shape=[shape(N, N), shape(N, NRHS), shape(ROWS_D...  18.1 us
    all_to_all x1, blocking collectives, over_far(): return lax.all_to_all(v, 'row', 0, 0, axis_index_groups=groups, tiled=True)  14.9 us
    pallas_call x1, Pallas kernels, terms(): pl.pallas_call(terms_body, out_shape=[shape(UNITS, TALL, NB)] * 2, grid=(...  12 us
    ppermute x2, starting transfers between devices, other_core(): return lax.ppermute(v, 'grp', [(i, i ^ 1) for i in range(8)])  7.52 us
    ppermute x2, waiting for transfers between devices, other_core(): return lax.ppermute(v, 'grp', [(i, i ^ 1) for i in range(8)])  5.51 us
  transfers between devices with their start and end apart: 2, of which 2 were waited for; matrix products, arithmetic and copies ran while one was open for 0% of the time, Pallas kernels for 0%

profile of v4, /device:TPU:1, one launch (start us, length us, event | category | flops | bytes accessed | tf_op | source)
XLA Modules:
  0.0 113.7 jit_solution(33486345852694919)
XLA Ops:
  0.6 12.0 %terms.1 = (f32[128,24,128]{2,1,0:T(8,128)S(1)}, f32[128,24,128]{2,1,0:T(8,128)S(1)}) custom-call(f32[2048,512]{1,0:T(8,128)} %refs_2_.1, f32[2048,128]{1,0:T(8,128)} %refs_3_.1, s32[16,128]{1,0:T(8,128)} %bitcast.5, s32[1,1024]{1,0:T(1,128)} %pick_ref.1), custom_call_target="tpu_custom_call" | custom-call | tf_op jit(solution)/shard_map/terms/pallas_call | solution.py:125
  12.6 3.3 %collective-permute-start = (f32[128,24,128]{2,1,0:T(8,128)S(1)}, f32[128,24,128]{2,1,0:T(8,128)S(1)}, u32[]{:S(2)}, u32[]{:S(2)}) collective-permute-start(f32[128,24,128]{2,1,0:T(8,128)S(1)} %get-tuple-element.6), channel_id=1, source_target_pairs={{0,32},{32,0},{64,96},{96,64},{128,160},{160,128},{192,224},{224,1... | collective-permute-start | bytes 4718600 | tf_op jit(solution)/shard_map/ppermute | solution.py:150
  15.9 3.0 %collective-permute-done = f32[128,24,128]{2,1,0:T(8,128)S(1)} collective-permute-done((f32[128,24,128]{2,1,0:T(8,128)S(1)}, f32[128,24,128]{2,1,0:T(8,128)S(1)}, u32[]{:S(2)}, u32[]{:S(2)}) %collective-permute-start) | collective-permute-done | bytes 1572896 | tf_op jit(solution)/shard_map/ppermute | solution.py:150
  18.9 0.2 add.3
  19.2 29.1 %all_to_all.15 = f32[32,4,24,128]{3,2,1,0:T(8,128)S(1)} all-to-all(f32[32,4,24,128]{3,2,1,0:T(8,128)S(1)} %bitcast.4), channel_id=1, replica_groups={{0,1,8,9,16,17,24,25,64,65,72,73,80,81,88,89,128,129,136,137,144,145,15..., dimensions={0} | all-to-all | bytes 3145728 | tf_op jit(solution)/shard_map/all_to_all | solution.py:163
  48.3 0.1 reduce_sum.18
  48.4 14.9 %all_to_all.16 = f32[4,4,24,128]{3,2,1,0:T(8,128)S(1)} all-to-all(f32[4,4,24,128]{3,2,1,0:T(8,128)S(1)} %broadcast_in_dim.6), channel_id=1, replica_groups={{0,2,4,6},{1,3,5,7},{8,10,12,14},{9,11,13,15},{16,18,20,22},{17,19,21,2..., dimensions={0} | all-to-all | bytes 393216 | tf_op jit(solution)/shard_map/all_to_all | solution.py:168
  63.3 0.2 broadcast_in_dim.7
  63.5 0.0 copy-start
  63.5 24.2 %all_to_all.17 = f32[32,4,24,128]{3,2,1,0:T(8,128)S(1)} all-to-all(f32[32,4,24,128]{3,2,1,0:T(8,128)S(1)} %broadcast_in_dim.7), channel_id=1, replica_groups={{0,1,8,9,16,17,24,25,64,65,72,73,80,81,88,89,128,129,136,137,144,145,15..., dimensions={0} | all-to-all | bytes 3145728 | tf_op jit(solution)/shard_map/all_to_all | solution.py:163
  87.6 0.0 copy-start.1
  87.6 1.1 gram.1.refs_0_
  88.7 4.2 %collective-permute-start.1 = (f32[2304,128]{1,0:T(8,128)S(1)}, f32[2304,128]{1,0:T(8,128)S(1)}, u32[]{:S(2)}, u32[]{:S(2)}) collective-permute-start(f32[2304,128]{1,0:T(8,128)S(1)} %gram.1.refs_0_), channel_id=1, source_target_pairs={{0,32},{32,0},{64,96},{96,64},{128,160},{160,128},{192,224},{224,1... | collective-permute-start | bytes 3538952 | tf_op jit(solution)/shard_map/ppermute | solution.py:150
  92.9 2.5 %collective-permute-done.1.refs_1_ = f32[2304,128]{1,0:T(8,128)S(1)} collective-permute-done((f32[2304,128]{1,0:T(8,128)S(1)}, f32[2304,128]{1,0:T(8,128)S(1)}, u32[]{:S(2)}, u32[]{:S(2)}) %collective-permute-start.1) | collective-permute-done | bytes 1179680 | tf_op jit(solution)/shard_map/ppermute | solution.py:150
  95.4 0.0 copy-done
  95.4 0.0 copy-done.1
  95.4 18.1 %finish.1 = (f32[512,512]{1,0:T(8,128)}, f32[512,128]{1,0:T(8,128)}, f32[2048,128]{1,0:T(8,128)}) custom-call(f32[2304,128]{1,0:T(8,128)S(1)} %gram.1.refs_0_, f32[2304,128]{1,0:T(8,128)S(1)} %collective-permute-done.1.refs_1_, f32[2048,512]{1,0:T(8,128)S(1)} %copy-done, f32[2048,128]{1,0:T(8,128)S(1)} %copy-done.1), custom_call_target="tpu_custom_call" | custom-call | tf_op jit(solution)/shard_map/finish/pallas_call | solution.py:374
  (2 shorter events, 0.0 us)
Async XLA Ops:
  12.6 6.3 %collective-permute-start = (f32[128,24,128]{2,1,0:T(8,128)S(1)}, f32[128,24,128]{2,1,0:T(8,128)S(1)}, u32[]{:S(2)}, u32[]{:S(2)}) collective-permute-start(f32[128,24,128]{2,1,0:T(8,128)S(1)} %get-tuple-element.6), channel_id=1, source_target_pairs={{0,32},{32,0},{64,96},{96,64},{128,160},{160,128},{192,224},{224,1... | collective-permute-start | bytes 4718600 | tf_op jit(solution)/shard_map/ppermute | solution.py:150
  63.5 31.9 %copy-start = (f32[2048,512]{1,0:T(8,128)S(1)}, f32[2048,512]{1,0:T(8,128)}, u32[]{:S(2)}) copy-start(f32[2048,512]{1,0:T(8,128)} %refs_2_.1) | copy-start | bytes 12582916
  87.6 7.8 %copy-start.1 = (f32[2048,128]{1,0:T(8,128)S(1)}, f32[2048,128]{1,0:T(8,128)}, u32[]{:S(2)}) copy-start(f32[2048,128]{1,0:T(8,128)} %refs_3_.1) | copy-start | bytes 3145732
  88.7 6.7 %collective-permute-start.1 = (f32[2304,128]{1,0:T(8,128)S(1)}, f32[2304,128]{1,0:T(8,128)S(1)}, u32[]{:S(2)}, u32[]{:S(2)}) collective-permute-start(f32[2304,128]{1,0:T(8,128)S(1)} %gram.1.refs_0_), channel_id=1, source_target_pairs={{0,32},{32,0},{64,96},{96,64},{128,160},{160,128},{192,224},{224,1... | collective-permute-start | bytes 3538952 | tf_op jit(solution)/shard_map/ppermute | solution.py:150

commit v5 on v4

--- a/solution.py
+++ b/solution.py
@@ -354,8 +354,8 @@
     x_ref[...] = x
     xs = jnp.concatenate(split(x), axis=1)
     puts = []
-    deep = ROWS_DEV // 4
-    for c in range(4):
+    deep = ROWS_DEV // 2
+    for c in range(2):
         rows = slice(c * deep, (c + 1) * deep)
         hi, lo = split(mat_ref[rows, :])
         ahead, behind = dot(hi, xs), dot(lo, xs)
@@ -376,7 +376,7 @@
         out_shape=[shape(N, N), shape(N, NRHS), shape(ROWS_DEV, NRHS)],
         in_specs=[vmem] * 4,
         out_specs=[vmem, vmem, hbm],
-        scratch_shapes=[V((N, N), F32)] * 5 + [V((N, NB), F32), V((ROWS_DEV, NRHS), F32), pltpu.SemaphoreType.DMA((4,))],
+        scratch_shapes=[V((N, N), F32)] * 5 + [V((N, NB), F32), V((ROWS_DEV, NRHS), F32), pltpu.SemaphoreType.DMA((2,))],
         compiler_params=pltpu.CompilerParams(vmem_limit_bytes=32 * MIB),
         name="finish",
     )(own, got, matrix, targets)

time: 114 us -> 114 us (level)
  no operation moved by 1% of the time
where the time goes in v5:
time: 114 us
  blocking collectives  68.1 us (60%)
  Pallas kernels  31.2 us (27%)
  starting transfers between devices  7.52 us (7%)
  waiting for transfers between devices  5.51 us (5%)
    all_to_all x2, blocking collectives, over_near(): lax.all_to_all(v, ('grp', 'row'), 0, 0, axis_index_groups=groups, tiled=T...  53.3 us
    pallas_call x1, Pallas kernels, finished(): pl.pallas_call(body, out_shape=[shape(N, N), shape(N, NRHS), shape(ROWS_D...  18.2 us
    all_to_all x1, blocking collectives, over_far(): return lax.all_to_all(v, 'row', 0, 0, axis_index_groups=groups, tiled=True)  14.9 us
    pallas_call x1, Pallas kernels, terms(): pl.pallas_call(terms_body, out_shape=[shape(UNITS, TALL, NB)] * 2, grid=(...  12 us
    ppermute x2, starting transfers between devices, other_core(): return lax.ppermute(v, 'grp', [(i, i ^ 1) for i in range(8)])  7.52 us
    ppermute x2, waiting for transfers between devices, other_core(): return lax.ppermute(v, 'grp', [(i, i ^ 1) for i in range(8)])  5.51 us
  transfers between devices with their start and end apart: 2, of which 2 were waited for; matrix products, arithmetic and copies ran while one was open for 0% of the time, Pallas kernels for 0%

profile of v5, /device:TPU:1, one launch (start us, length us, event | category | flops | bytes accessed | tf_op | source)
XLA Modules:
  0.0 113.7 jit_solution(7819540320888674412)
XLA Ops:
  0.6 12.0 %terms.1 = (f32[128,24,128]{2,1,0:T(8,128)S(1)}, f32[128,24,128]{2,1,0:T(8,128)S(1)}) custom-call(f32[2048,512]{1,0:T(8,128)} %refs_2_.1, f32[2048,128]{1,0:T(8,128)} %refs_3_.1, s32[16,128]{1,0:T(8,128)} %bitcast.5, s32[1,1024]{1,0:T(1,128)} %pick_ref.1), custom_call_target="tpu_custom_call" | custom-call | tf_op jit(solution)/shard_map/terms/pallas_call | solution.py:125
  12.6 3.3 %collective-permute-start = (f32[128,24,128]{2,1,0:T(8,128)S(1)}, f32[128,24,128]{2,1,0:T(8,128)S(1)}, u32[]{:S(2)}, u32[]{:S(2)}) collective-permute-start(f32[128,24,128]{2,1,0:T(8,128)S(1)} %get-tuple-element.6), channel_id=1, source_target_pairs={{0,32},{32,0},{64,96},{96,64},{128,160},{160,128},{192,224},{224,1... | collective-permute-start | bytes 4718600 | tf_op jit(solution)/shard_map/ppermute | solution.py:150
  15.9 3.0 %collective-permute-done = f32[128,24,128]{2,1,0:T(8,128)S(1)} collective-permute-done((f32[128,24,128]{2,1,0:T(8,128)S(1)}, f32[128,24,128]{2,1,0:T(8,128)S(1)}, u32[]{:S(2)}, u32[]{:S(2)}) %collective-permute-start) | collective-permute-done | bytes 1572896 | tf_op jit(solution)/shard_map/ppermute | solution.py:150
  18.9 0.2 add.3
  19.2 29.1 %all_to_all.15 = f32[32,4,24,128]{3,2,1,0:T(8,128)S(1)} all-to-all(f32[32,4,24,128]{3,2,1,0:T(8,128)S(1)} %bitcast.4), channel_id=1, replica_groups={{0,1,8,9,16,17,24,25,64,65,72,73,80,81,88,89,128,129,136,137,144,145,15..., dimensions={0} | all-to-all | bytes 3145728 | tf_op jit(solution)/shard_map/all_to_all | solution.py:163
  48.3 0.1 reduce_sum.18
  48.4 14.9 %all_to_all.16 = f32[4,4,24,128]{3,2,1,0:T(8,128)S(1)} all-to-all(f32[4,4,24,128]{3,2,1,0:T(8,128)S(1)} %broadcast_in_dim.6), channel_id=1, replica_groups={{0,2,4,6},{1,3,5,7},{8,10,12,14},{9,11,13,15},{16,18,20,22},{17,19,21,2..., dimensions={0} | all-to-all | bytes 393216 | tf_op jit(solution)/shard_map/all_to_all | solution.py:168
  63.3 0.2 broadcast_in_dim.7
  63.5 0.0 copy-start
  63.5 24.2 %all_to_all.17 = f32[32,4,24,128]{3,2,1,0:T(8,128)S(1)} all-to-all(f32[32,4,24,128]{3,2,1,0:T(8,128)S(1)} %broadcast_in_dim.7), channel_id=1, replica_groups={{0,1,8,9,16,17,24,25,64,65,72,73,80,81,88,89,128,129,136,137,144,145,15..., dimensions={0} | all-to-all | bytes 3145728 | tf_op jit(solution)/shard_map/all_to_all | solution.py:163
  87.6 0.0 copy-start.1
  87.6 1.1 gram.1.refs_0_
  88.7 4.2 %collective-permute-start.1 = (f32[2304,128]{1,0:T(8,128)S(1)}, f32[2304,128]{1,0:T(8,128)S(1)}, u32[]{:S(2)}, u32[]{:S(2)}) collective-permute-start(f32[2304,128]{1,0:T(8,128)S(1)} %gram.1.refs_0_), channel_id=1, source_target_pairs={{0,32},{32,0},{64,96},{96,64},{128,160},{160,128},{192,224},{224,1... | collective-permute-start | bytes 3538952 | tf_op jit(solution)/shard_map/ppermute | solution.py:150
  92.9 2.5 %collective-permute-done.1.refs_1_ = f32[2304,128]{1,0:T(8,128)S(1)} collective-permute-done((f32[2304,128]{1,0:T(8,128)S(1)}, f32[2304,128]{1,0:T(8,128)S(1)}, u32[]{:S(2)}, u32[]{:S(2)}) %collective-permute-start.1) | collective-permute-done | bytes 1179680 | tf_op jit(solution)/shard_map/ppermute | solution.py:150
  95.4 0.0 copy-done
  95.4 0.0 copy-done.1
  95.4 18.2 %finish.1 = (f32[512,512]{1,0:T(8,128)}, f32[512,128]{1,0:T(8,128)}, f32[2048,128]{1,0:T(8,128)}) custom-call(f32[2304,128]{1,0:T(8,128)S(1)} %gram.1.refs_0_, f32[2304,128]{1,0:T(8,128)S(1)} %collective-permute-done.1.refs_1_, f32[2048,512]{1,0:T(8,128)S(1)} %copy-done, f32[2048,128]{1,0:T(8,128)S(1)} %copy-done.1), custom_call_target="tpu_custom_call" | custom-call | tf_op jit(solution)/shard_map/finish/pallas_call | solution.py:374
  (2 shorter events, 0.0 us)
Async XLA Ops:
  12.6 6.3 %collective-permute-start = (f32[128,24,128]{2,1,0:T(8,128)S(1)}, f32[128,24,128]{2,1,0:T(8,128)S(1)}, u32[]{:S(2)}, u32[]{:S(2)}) collective-permute-start(f32[128,24,128]{2,1,0:T(8,128)S(1)} %get-tuple-element.6), channel_id=1, source_target_pairs={{0,32},{32,0},{64,96},{96,64},{128,160},{160,128},{192,224},{224,1... | collective-permute-start | bytes 4718600 | tf_op jit(solution)/shard_map/ppermute | solution.py:150
  63.5 31.9 %copy-start = (f32[2048,512]{1,0:T(8,128)S(1)}, f32[2048,512]{1,0:T(8,128)}, u32[]{:S(2)}) copy-start(f32[2048,512]{1,0:T(8,128)} %refs_2_.1) | copy-start | bytes 12582916
  87.6 7.8 %copy-start.1 = (f32[2048,128]{1,0:T(8,128)S(1)}, f32[2048,128]{1,0:T(8,128)}, u32[]{:S(2)}) copy-start(f32[2048,128]{1,0:T(8,128)} %refs_3_.1) | copy-start | bytes 3145732
  88.7 6.7 %collective-permute-start.1 = (f32[2304,128]{1,0:T(8,128)S(1)}, f32[2304,128]{1,0:T(8,128)S(1)}, u32[]{:S(2)}, u32[]{:S(2)}) collective-permute-start(f32[2304,128]{1,0:T(8,128)S(1)} %gram.1.refs_0_), channel_id=1, source_target_pairs={{0,32},{32,0},{64,96},{96,64},{128,160},{160,128},{192,224},{224,1... | collective-permute-start | bytes 3538952 | tf_op jit(solution)/shard_map/ppermute | solution.py:150
